TPU v7x, 32 devices: a whole 2x2x4 slice. The times are simulated.
32 devices in a mesh: groups: 2 (over y), seq: 4 (over z), blk: 2 (over x), chan: 2 (over core).
Axes of the slice: x: 2, y: 2, z: 4, core: 2. Of those that a mesh axis runs over, the one named last changes fastest.
Arguments:
- queries: bfloat16 [4, 8, 32, 4096], P(('groups', 'blk'), 'seq', 'chan'), parts along dimension 0, may hold values from -8 to 8
- keys: bfloat16 [4, 8, 32, 4096], P(('groups', 'blk'), 'seq', 'chan'), parts along dimension 0, may hold values from -8 to 8
- values: bfloat16 [4, 8, 32, 4096], P(('groups', 'blk'), 'seq', 'chan'), parts along dimension 0, may hold values from -16 to 16
- norm_gain: float32 [4096], replicated, may hold values from 0.1 to 1.9
- head_weight: bfloat16 [4096, 64], replicated, may hold values from -0.09375 to 0.09375
- head_bias: float32 [64], replicated, may hold values from -3 to 3
- in_weight: bfloat16 [3, 3, 64, 512], replicated, may hold values from -0.25 to 0.25
- in_bias: float32 [512], replicated, may hold values from -3 to 3
- conv_weight: bfloat16 [3, 3, 512, 512], P(None, None, None, 'chan'), may hold values from -0.15625 to 0.15625
- conv_bias: float32 [512], P('chan'), may hold values from -3 to 3
Outputs:
- decoded: bfloat16 [4, 8, 32, 512], P(('groups', 'blk'), 'seq', None, 'chan'), parts along dimension 0
There are 2 independent parts, one for each index of `groups`. A program takes and returns all parts, laid end to end along the dimension named above; an argument that names none is the same for every part. Nothing has to cross between parts.
All inputs are finite; a program needn't handle non-finite values.
Results may differ from a plain program's by a relative error of at most 0.025.
Values may be sent and summed in bfloat16 or wider, within the bound.
No kernel may reach another device: no remote copies, remote signals or barrier semaphores. Data moves between devices by JAX's collectives and lax.ppermute only.
A program may use at most 64 MiB of HBM per device.

v0:
```python
import jax
import jax.numpy as jnp
from jax import lax
from jax.sharding import PartitionSpec as P

HD = 128
epsilon = 1e-06


def with_halo(cells, sides, width):
    for axis, dim in sides:
        count = lax.axis_size(axis)
        ends = count - 1
        head = lax.slice_in_dim(cells, 0, width, axis=dim)
        tail = lax.slice_in_dim(cells, cells.shape[dim] - width, cells.shape[dim], axis=dim)
        cells = jnp.concatenate(
            [
                lax.ppermute(tail, axis, [(i, (i + 1) % count) for i in range(ends)]),
                cells,
                lax.ppermute(head, axis, [((i + 1) % count, i) for i in range(ends)]),
            ],
            axis=dim,
        )
    return cells


def conv_valid(inputs, kernel):
    col_count = inputs.shape[2]
    padded = jnp.pad(inputs, ((0, 0), (0, 0), (1, 1), (0, 0)))
    stacked = jnp.concatenate(
        [padded[:, :, col_tap : col_tap + col_count, :] for col_tap in range(3)], axis=-1
    )
    rows_out = inputs.shape[1] - 2
    result = None
    for row_tap in range(3):
        flat_kernel = kernel[row_tap].reshape(3 * kernel.shape[2], kernel.shape[3])
        term = jnp.einsum(
            "frci,io->frco",
            stacked[:, row_tap : row_tap + rows_out],
            flat_kernel,
            preferred_element_type=jnp.float32,
        )
        result = term if result is None else result + term
    return result


def absorb(running, key_block, value_block, query_heads, score_scale):
    run_max, denoms, numers = running
    scores = (
        jnp.einsum("hqd,hkd->hqk", query_heads, key_block, preferred_element_type=jnp.float32)
        * score_scale
    )
    fresh_max = jnp.maximum(run_max, jnp.max(scores, axis=-1))
    rescale = jnp.exp(run_max - fresh_max)
    expo = jnp.exp(scores - fresh_max[..., None])
    denoms = denoms * rescale + jnp.sum(expo, axis=-1)
    numers = numers * rescale[..., None] + jnp.einsum(
        "hqk,hkd->hqd", expo.astype(jnp.bfloat16), value_block, preferred_element_type=jnp.float32
    )
    return (fresh_max, denoms, numers)


def per_device(
    queries,
    keys,
    values,
    norm_gain,
    head_weight,
    head_bias,
    in_weight,
    in_bias,
    conv_weight,
    conv_bias,
):
    frame_dev, rows_dev, cols_dev, feat = queries.shape
    seq_count = lax.axis_size("seq")
    feat_dev = feat // seq_count
    heads_dev = feat_dev // HD
    score_scale = HD ** (-0.5)
    query_all, key_all, value_all = (
        lax.all_to_all(queries, "seq", split_axis=3, concat_axis=1, tiled=True),
        lax.all_to_all(keys, "seq", split_axis=3, concat_axis=1, tiled=True),
        lax.all_to_all(values, "seq", split_axis=3, concat_axis=1, tiled=True),
    )
    all_rows = query_all.shape[1]

    def to_heads(block):
        return block.reshape(-1, heads_dev, HD).transpose(1, 0, 2)

    query_heads = to_heads(query_all)
    key_heads = to_heads(key_all)
    value_heads = to_heads(value_all)
    token_local = query_heads.shape[1]

    def attend_piece(running, block_pair):
        key_piece, value_piece = block_pair
        key_rows = key_piece.shape[1]
        if key_rows > 1024 and key_rows % 1024 == 0:
            count = key_rows // 1024
            key_split = key_piece.reshape(heads_dev, count, 1024, HD).transpose(1, 0, 2, 3)
            value_split = value_piece.reshape(heads_dev, count, 1024, HD).transpose(1, 0, 2, 3)

            def step_block(state, pair_block):
                return (absorb(state, pair_block[0], pair_block[1], query_heads, score_scale), None)

            running, _ = lax.scan(step_block, running, (key_split, value_split))
            return running
        return absorb(running, key_piece, value_piece, query_heads, score_scale)

    start_state = (
        jnp.full((heads_dev, token_local), -1e30, jnp.float32),
        jnp.zeros((heads_dev, token_local), jnp.float32),
        jnp.zeros((heads_dev, token_local, HD), jnp.float32),
    )
    run_max, denoms, numers = attend_piece(
        start_state,
        (
            lax.all_gather(key_heads, ("blk", "chan"), axis=1, tiled=True),
            lax.all_gather(value_heads, ("blk", "chan"), axis=1, tiled=True),
        ),
    )
    attended = (numers / denoms[..., None]).astype(jnp.bfloat16)
    attended = attended.transpose(1, 0, 2).reshape(frame_dev, all_rows, cols_dev, feat_dev)
    back = lax.all_to_all(attended, "seq", split_axis=1, concat_axis=3, tiled=True)
    wide_att = back.astype(jnp.float32)
    squares = jnp.sum(wide_att * wide_att, axis=-1)
    normed = (wide_att * norm_gain).astype(jnp.bfloat16)
    projected = jnp.einsum("frcd,dl->frcl", normed, head_weight, preferred_element_type=jnp.float32)
    rms = jnp.sqrt(squares / feat + epsilon)
    latent_cols = (projected / rms[..., None] + head_bias).astype(jnp.bfloat16)
    latent = lax.all_gather(latent_cols, "chan", axis=2, tiled=True)
    wide_rows = with_halo(latent, (("seq", 1),), 2)
    pre_act = conv_valid(wide_rows, in_weight) + in_bias
    row_ids = lax.axis_index("seq") * rows_dev - 1 + jnp.arange(rows_dev + 2, dtype=jnp.int32)
    inside = (row_ids >= 0) & (row_ids < rows_dev * seq_count)
    activation = jnp.where(inside[None, :, None, None], jax.nn.silu(pre_act), 0.0).astype(
        jnp.bfloat16
    )
    decoded = (conv_valid(activation, conv_weight) + conv_bias).astype(jnp.bfloat16)
    return decoded


def solution(mesh):
    return jax.shard_map(
        per_device,
        mesh=mesh,
        in_specs=(
            P(("groups", "blk"), "seq", "chan", None),
            P(("groups", "blk"), "seq", "chan", None),
            P(("groups", "blk"), "seq", "chan", None),
            P(),
            P(),
            P(),
            P(),
            P(),
            P(None, None, None, "chan"),
            P("chan"),
        ),
        out_specs=P(("groups", "blk"), "seq", None, "chan"),
        check_vma=False,
    )
```

profile of v0, /device:TPU:0, one launch (start us, length us, event | category | flops | bytes accessed | tf_op | source)
XLA Modules:
  0.0 111.8 jit_solution(7479379873750700301)
XLA Ops:
  6.5 4.5 %copy.29 = bf16[1,2,16,4096]{2,1,0,3:T(2,128)(2,1)S(1)} copy(bf16[1,2,16,4096]{3,2,1,0:T(8,128)(2,1)} %param.11) | data formatting | bytes 524288 | tf_op args[1]
  11.1 2.2 %reshape.143 = bf16[4,2,16384]{2,1,0:T(2,128)(2,1)S(1)} reshape(bf16[4096,1,2,16]{3,2,1,0:T(2,128)(2,1)S(1)} %bitcast.113) | data formatting | bytes 524288
  13.3 15.0 %all_to_all.54 = bf16[4,2,16384]{2,1,0:T(2,128)(2,1)S(1)} all-to-all(bf16[4,2,16384]{2,1,0:T(2,128)(2,1)S(1)} %reshape.143), channel_id=1, replica_groups=mesh['groups'=2,'seq'=4,'blk'=2,'chan'=2] {'seq'}, dimensions={0} | all-to-all | bytes 524288 | tf_op jit(solution)/shard_map/all_to_all | solution.py:82
  28.3 1.4 %reshape.144 = bf16[4096,1,2,16]{3,2,1,0:T(2,128)(2,1)S(1)} reshape(bf16[4,2,16384]{2,1,0:T(2,128)(2,1)S(1)} %all_to_all.54) | data formatting | bytes 524288
  29.8 1.3 %copy.30 = bf16[1,2,16,4,1024]{4,2,1,3,0:T(8,128)(2,1)S(1)} copy(bf16[1,2,16,4,1024]{2,1,4,3,0:T(2,128)(2,1)S(1)} %bitcast.110) | data formatting | bytes 524288 | tf_op jit(solution)/shard_map/all_to_all | solution.py:82
  31.1 0.7 copy.51
  31.8 0.0 all-gather.4.cloned.1.call-update
  31.8 0.0 all-gather.6.cloned.1.call-start
  31.9 2.7 %copy.32 = bf16[1,2,16,4096]{2,1,0,3:T(2,128)(2,1)S(1)} copy(bf16[1,2,16,4096]{3,2,1,0:T(8,128)(2,1)S(1)} %copy-done.1) | data formatting | bytes 524288 | tf_op args[2]
  34.7 2.2 %reshape.141 = bf16[4,2,16384]{2,1,0:T(2,128)(2,1)S(1)} reshape(bf16[4096,1,2,16]{3,2,1,0:T(2,128)(2,1)S(1)} %bitcast.114) | data formatting | bytes 524288
  36.9 11.0 %all_to_all.55 = bf16[4,2,16384]{2,1,0:T(2,128)(2,1)S(1)} all-to-all(bf16[4,2,16384]{2,1,0:T(2,128)(2,1)S(1)} %reshape.141), channel_id=1, replica_groups=mesh['groups'=2,'seq'=4,'blk'=2,'chan'=2] {'seq'}, dimensions={0} | all-to-all | bytes 524288 | tf_op jit(solution)/shard_map/all_to_all | solution.py:83
  47.8 1.4 %reshape.142 = bf16[4096,1,2,16]{3,2,1,0:T(2,128)(2,1)S(1)} reshape(bf16[4,2,16384]{2,1,0:T(2,128)(2,1)S(1)} %all_to_all.55) | data formatting | bytes 524288
  49.3 1.3 %copy.33 = bf16[1,2,16,4,1024]{4,2,1,3,0:T(8,128)(2,1)S(1)} copy(bf16[1,2,16,4,1024]{2,1,4,3,0:T(2,128)(2,1)S(1)} %bitcast.111) | data formatting | bytes 524288 | tf_op jit(solution)/shard_map/all_to_all | solution.py:83
  50.6 0.7 copy.50
  51.4 2.7 %copy.26 = bf16[1,2,16,4096]{2,1,0,3:T(2,128)(2,1)S(1)} copy(bf16[1,2,16,4096]{3,2,1,0:T(8,128)(2,1)S(1)} %copy-done.2) | data formatting | bytes 524288 | tf_op args[0]
  54.1 2.2 %reshape.145 = bf16[4,2,16384]{2,1,0:T(2,128)(2,1)S(1)} reshape(bf16[4096,1,2,16]{3,2,1,0:T(2,128)(2,1)S(1)} %bitcast.115) | data formatting | bytes 524288
  56.3 11.0 %all_to_all.56 = bf16[4,2,16384]{2,1,0:T(2,128)(2,1)S(1)} all-to-all(bf16[4,2,16384]{2,1,0:T(2,128)(2,1)S(1)} %reshape.145), channel_id=1, replica_groups=mesh['groups'=2,'seq'=4,'blk'=2,'chan'=2] {'seq'}, dimensions={0} | all-to-all | bytes 524288 | tf_op jit(solution)/shard_map/all_to_all | solution.py:81
  67.3 1.4 %reshape.146 = bf16[4096,1,2,16]{3,2,1,0:T(2,128)(2,1)S(1)} reshape(bf16[4,2,16384]{2,1,0:T(2,128)(2,1)S(1)} %all_to_all.56) | data formatting | bytes 524288
  68.7 1.3 %copy.27 = bf16[1,2,16,4,1024]{4,2,1,3,0:T(8,128)(2,1)S(1)} copy(bf16[1,2,16,4,1024]{2,1,4,3,0:T(2,128)(2,1)S(1)} %bitcast.112) | data formatting | bytes 524288 | tf_op jit(solution)/shard_map/all_to_all | solution.py:81
  70.1 0.0 all-gather.4.cloned.1.call-done
  70.1 1.7 %multiply_reduce_fusion = (f32[8,128]{1,0:T(8,128)S(1)}, f32[8,128,512]{2,1,0:T(8,128)S(1)}) fusion(bf16[8,512,128]{2,1,0:T(8,128)(2,1)} %all-gather.4.cloned.1.call-done, bf16[128,8,128]{2,1,0:T(8,128)(2,1)S(1)} %bitcast.127), kind=kOutput, calls=%fused_computation.1 | convolution fusion | flops 135265280 | bytes 3411968 | tf_op jit(solution)/shard_map/hqd,hkd->hqk/dot_general | solution.py:50
  71.8 0.6 fusion
  72.4 0.0 all-gather.6.cloned.1.call-done
  72.5 1.9 %fusion.4 = bf16[128,8,128]{2,0,1:T(8,128)(2,1)S(1)} fusion(bf16[8,512,128]{2,1,0:T(8,128)(2,1)} %all-gather.6.cloned.1.call-done, f32[8,128,512]{2,1,0:T(8,128)S(1)} %get-tuple-element.18, f32[8,128]{1,0:T(8,128)S(1)} %get-tuple-element.16, f32[128,8]{0,1:T(8,128)S(1)} %bitcast_add_fusion, f32[128,8]{0,1:T(8,128)S(1)} %get-tuple-element.15), kind=kOutput, calls=%fused_computation.7 | convolution fusion | flops 136183808 | bytes 3420160 | tf_op jit(solution)/shard_map/hqk,hkd->hqd/dot_general | solution.py:57
  74.4 0.2 copy.35
  74.6 0.8 reshape.124
  75.4 3.4 %all-to-all-start.3 = ((bf16[1,8,16,1024]{3,2,0,1:T(8,128)(2,1)}), bf16[1,8,16,1024]{3,2,0,1:T(8,128)(2,1)S(1)}, u32[]{:S(2)}, u32[]{:S(2)}) async-start(bf16[1,8,16,1024]{3,2,0,1:T(8,128)(2,1)} %bitcast.12), calls=%async_computation.3 | async-start | bytes 524288 | tf_op jit(solution)/shard_map/all_to_all | solution.py:124
  78.8 1.8 %fusion.30 = (bf16[1,3,64,512]{3,2,1,0:T(8,128)(2,1)}, bf16[1,3,64,512]{3,2,1,0:T(8,128)(2,1)S(1)}, bf16[1,3,64,512]{3,2,1,0:T(8,128)(2,1)S(1)}) fusion(bf16[3,3,64,512]{3,2,1,0:T(8,128)(2,1)} %param.16), kind=kLoop, calls=%fused_computation.60 | loop fusion | bytes 1179648 | tf_op jit(solution)/shard_map/slice | solution.py:36
  80.6 1.8 %fusion.29 = (bf16[1,3,512,256]{3,2,1,0:T(8,128)(2,1)S(1)}, bf16[1,3,512,256]{3,2,1,0:T(8,128)(2,1)S(1)}, bf16[1,3,512,256]{3,2,1,0:T(8,128)(2,1)S(1)}) fusion(bf16[3,3,512,256]{3,2,1,0:T(8,128)(2,1)} %param.18), kind=kLoop, calls=%fused_computation.59 | loop fusion | bytes 4718592 | tf_op jit(solution)/shard_map/slice | solution.py:36
  82.4 4.3 %all-to-all-done.3 = bf16[1,8,16,1024]{3,2,0,1:T(8,128)(2,1)S(1)} async-done(((bf16[1,8,16,1024]{3,2,0,1:T(8,128)(2,1)}), bf16[1,8,16,1024]{3,2,0,1:T(8,128)(2,1)S(1)}, u32[]{:S(2)}, u32[]{:S(2)}) %all-to-all-start.3) | async-done | bytes 262176 | tf_op jit(solution)/shard_map/all_to_all | solution.py:124
  86.8 1.1 %copy.38 = f32[1,2,16,4,1024]{4,3,2,1,0:T(4,128)} copy(f32[1,2,16,4,1024]{4,2,1,3,0:T(8,128)S(1)} %bitcast.119) | data formatting | bytes 1048576 | tf_op jit(solution)/shard_map/convert_element_type | solution.py:125
  87.9 2.2 %reshape.131 = f32[2,16,4096]{2,1,0:T(8,128)} reshape(f32[1,2,16,4,1024]{4,3,2,1,0:T(4,128)} %copy.38) | data formatting | bytes 1048576 | tf_op jit(solution)/shard_map/convert_element_type | solution.py:125
  90.1 0.7 multiply_reduce_fusion.1
  90.8 0.7 reduce_sum.31
  91.6 1.4 %fusion.10 = bf16[2,16,64]{2,1,0:T(8,128)(2,1)S(1)} fusion(bf16[4096,64]{0,1:T(8,128)(2,1)S(1)} %copy-done, f32[2,16,4096]{2,1,0:T(8,128)} %reshape.131, f32[4096]{0:T(1024)S(1)} %copy-done.4, f32[64]{0:T(128)} %param.15, f32[2,16]{1,0:T(2,128)S(1)} %add_sqrt_fusion), kind=kOutput, calls=%fused_computation.18 | convolution fusion | flops 17045504 | bytes 1069440 | tf_op jit(solution)/shard_map/frcd,dl->frcl/dot_general | solution.py:128
  93.0 1.8 %all-gather = bf16[2,32,64]{2,1,0:T(8,128)(2,1)S(1)} all-gather(bf16[2,16,64]{2,1,0:T(8,128)(2,1)S(1)} %fusion.10), channel_id=2, replica_groups=mesh['groups'=2,'seq'=4,'blk'=2,'chan'=2] {'chan'}, dimensions={1}, use_global_device_ids=true | all-gather | bytes 12288 | tf_op jit(solution)/shard_map/all_gather | solution.py:131
  94.8 2.2 %collective-permute-start = (bf16[1,2,32,64]{3,2,1,0:T(8,128)(2,1)S(1)}, bf16[1,2,32,64]{3,2,1,0:T(8,128)(2,1)S(1)}, u32[]{:S(2)}, u32[]{:S(2)}) collective-permute-start(bf16[1,2,32,64]{3,2,1,0:T(8,128)(2,1)S(1)} %bitcast.131), channel_id=1, source_target_pairs={{0,4},{4,8},{8,12},{1,5},{5,9},{9,13},{2,6},{6,10},{10,14},{3,7},{... | collective-permute-start | bytes 24584 | tf_op jit(solution)/shard_map/ppermute | solution.py:18
  97.0 1.3 %collective-permute-start.1 = (bf16[1,2,32,64]{3,2,1,0:T(8,128)(2,1)S(1)}, bf16[1,2,32,64]{3,2,1,0:T(8,128)(2,1)S(1)}, u32[]{:S(2)}, u32[]{:S(2)}) collective-permute-start(bf16[1,2,32,64]{3,2,1,0:T(8,128)(2,1)S(1)} %bitcast.132), channel_id=1, source_target_pairs={{4,0},{8,4},{12,8},{5,1},{9,5},{13,9},{6,2},{10,6},{14,10},{7,3},{... | collective-permute-start | bytes 24584 | tf_op jit(solution)/shard_map/ppermute | solution.py:20
  98.3 0.1 collective-permute-done
  98.5 4.2 %collective-permute-done.1 = bf16[1,2,32,64]{3,2,1,0:T(8,128)(2,1)S(1)} collective-permute-done((bf16[1,2,32,64]{3,2,1,0:T(8,128)(2,1)S(1)}, bf16[1,2,32,64]{3,2,1,0:T(8,128)(2,1)S(1)}, u32[]{:S(2)}, u32[]{:S(2)}) %collective-permute-start.1) | collective-permute-done | bytes 8224 | tf_op jit(solution)/shard_map/ppermute | solution.py:20
  102.7 0.1 pad_maximum_fusion.1
  102.8 0.2 fusion.25
  103.0 0.2 convolution_add_fusion.1
  103.2 0.2 fusion.18
  103.5 0.1 pad_slice_fusion.1
  103.6 0.3 fusion.20
  103.8 0.3 convolution_add_fusion.3
  104.1 0.9 fusion.8
  (27 shorter events, 0.4 us)
Async XLA Ops:
  6.5 85.0 %copy-start = (bf16[4096,64]{0,1:T(8,128)(2,1)S(1)}, bf16[4096,64]{0,1:T(8,128)(2,1)}, u32[]{:S(2)}) copy-start(bf16[4096,64]{0,1:T(8,128)(2,1)} %param.14) | copy-start | bytes 1572868
  6.5 63.5 %all-gather.4.cloned.1.call-start = ((), (), s32[]{:S(2)}) async-start(), calls=%async_computation.4 | async-start | bytes 1310720 | tf_op jit(solution)/shard_map/all_gather | solution.py:118
  29.8 2.1 %copy-start.1 = (bf16[1,2,16,4096]{3,2,1,0:T(8,128)(2,1)S(1)}, bf16[1,2,16,4096]{3,2,1,0:T(8,128)(2,1)}, u32[]{:S(2)}) copy-start(bf16[1,2,16,4096]{3,2,1,0:T(8,128)(2,1)} %param.12) | copy-start | bytes 786436
  31.8 40.6 %all-gather.6.cloned.1.call-start = ((), (), s32[]{:S(2)}) async-start(), calls=%async_computation.5 | async-start | bytes 1310720 | tf_op jit(solution)/shard_map/all_gather | solution.py:119
  49.3 2.1 %copy-start.2 = (bf16[1,2,16,4096]{3,2,1,0:T(8,128)(2,1)S(1)}, bf16[1,2,16,4096]{3,2,1,0:T(8,128)(2,1)}, u32[]{:S(2)}) copy-start(bf16[1,2,16,4096]{3,2,1,0:T(8,128)(2,1)} %param.10) | copy-start | bytes 786436
  75.4 11.4 %all-to-all-start.3 = ((bf16[1,8,16,1024]{3,2,0,1:T(8,128)(2,1)}), bf16[1,8,16,1024]{3,2,0,1:T(8,128)(2,1)S(1)}, u32[]{:S(2)}, u32[]{:S(2)}) async-start(bf16[1,8,16,1024]{3,2,0,1:T(8,128)(2,1)} %bitcast.12), calls=%async_computation.3 | async-start | bytes 524288 | tf_op jit(solution)/shard_map/all_to_all | solution.py:124
  82.4 9.2 %copy-start.4 = (f32[4096]{0:T(1024)S(1)}, f32[4096]{0:T(1024)}, u32[]{:S(2)}) copy-start(f32[4096]{0:T(1024)} %param.13) | copy-start | bytes 49156
  90.8 12.4 %copy-start.6 = (f32[512]{0:T(512)S(1)}, f32[512]{0:T(512)}, u32[]{:S(2)}) copy-start(f32[512]{0:T(512)} %param.17) | copy-start | bytes 6148
  91.6 11.7 %copy-start.3 = (bf16[1,3,64,512]{3,2,1,0:T(8,128)(2,1)S(1)}, bf16[1,3,64,512]{3,2,1,0:T(8,128)(2,1)}, u32[]{:S(2)}) copy-start(bf16[1,3,64,512]{3,2,1,0:T(8,128)(2,1)} %get-tuple-element.8) | copy-start | bytes 589828
  94.8 3.7 %collective-permute-start = (bf16[1,2,32,64]{3,2,1,0:T(8,128)(2,1)S(1)}, bf16[1,2,32,64]{3,2,1,0:T(8,128)(2,1)S(1)}, u32[]{:S(2)}, u32[]{:S(2)}) collective-permute-start(bf16[1,2,32,64]{3,2,1,0:T(8,128)(2,1)S(1)} %bitcast.131), channel_id=1, source_target_pairs={{0,4},{4,8},{8,12},{1,5},{5,9},{9,13},{2,6},{6,10},{10,14},{3,7},{... | collective-permute-start | bytes 24584 | tf_op jit(solution)/shard_map/ppermute | solution.py:18
  97.0 5.6 %collective-permute-start.1 = (bf16[1,2,32,64]{3,2,1,0:T(8,128)(2,1)S(1)}, bf16[1,2,32,64]{3,2,1,0:T(8,128)(2,1)S(1)}, u32[]{:S(2)}, u32[]{:S(2)}) collective-permute-start(bf16[1,2,32,64]{3,2,1,0:T(8,128)(2,1)S(1)} %bitcast.132), channel_id=1, source_target_pairs={{4,0},{8,4},{12,8},{5,1},{9,5},{13,9},{6,2},{10,6},{14,10},{7,3},{... | collective-permute-start | bytes 24584 | tf_op jit(solution)/shard_map/ppermute | solution.py:20
  103.2 0.9 copy-start.5
Sparse Core Ops, SparseCore 0:
  32.0 15.7 all-gather.3
  51.5 15.7 all-gather.5
where the time goes:
time: 113 us; the launch traced here: 112 us
  blocking collectives  38.8 us (34%)
  local copies, waits for them, and re-layouts  34.3 us (30%)
  between operations  13.8 us (12%)
  waiting for transfers between devices  8.74 us (8%)
  matrix products  7.01 us (6%)
  starting transfers between devices  6.99 us (6%)
  other arithmetic  2.25 us (2%)
    unnamed x26, local copies, waits for them, and re-layouts  21.1 us
    all_to_all x1, blocking collectives, per_device(): lax.all_to_all(keys, 'seq', split_axis=3, concat_axis=1, tiled=True)  15 us
    all_to_all x1, blocking collectives, per_device(): lax.all_to_all(values, 'seq', split_axis=3, concat_axis=1, tiled=True)  11 us
    all_to_all x1, blocking collectives, per_device(): lax.all_to_all(queries, 'seq', split_axis=3, concat_axis=1, tiled=True)  11 us
    all_to_all x1, waiting for transfers between devices, per_device(): lax.all_to_all(attended, 'seq', split_axis=1, concat_axis=3, tiled=True)  4.35 us
    ppermute x1, waiting for transfers between devices, with_halo(): lax.ppermute(head, axis, [((i + 1) % count, i) for i in range(ends)])  4.21 us
    slice x2, local copies, waits for them, and re-layouts, conv_valid(): flat_kernel = kernel[row_tap].reshape(3 * kernel.shape[2], kernel.shape[3])  3.6 us
    all_to_all x1, starting transfers between devices, per_device(): lax.all_to_all(attended, 'seq', split_axis=1, concat_axis=3, tiled=True)  3.4 us
  transfers between devices with their start and end apart: 5, of which 3 were waited for; matrix products, arithmetic and copies ran while one was open for 20% of the time, Pallas kernels for 0%

commit v1 on v0

--- a/solution.py
+++ b/solution.py
@@ -80,7 +80,10 @@
     query_all, key_all, value_all = (
         lax.all_to_all(queries, "seq", split_axis=3, concat_axis=1, tiled=True),
         lax.all_to_all(keys, "seq", split_axis=3, concat_axis=1, tiled=True),
-        lax.all_to_all(values, "seq", split_axis=3, concat_axis=1, tiled=True),
+        jnp.concatenate(
+            lax.all_to_all(jnp.stack(jnp.split(values, lax.axis_size("seq"), axis=3)), "seq", 0, 0),
+            axis=1,
+        ),
     )
     all_rows = query_all.shape[1]
 

time: 113 us -> 109 us (0.965)
  local copies, waits for them, and re-layouts: 34.3 us -> 26.7 us
  waiting for transfers between devices: 8.74 us -> 11.3 us
    unnamed x26 -> x23, local copies, waits for them, and re-layouts: 21.1 us -> 14.7 us
    all_to_all x1, waiting for transfers between devices: 4.35 us -> 5.68 us  [per_device(): lax.all_to_all(attended, 'seq', split_axis=1, concat_axis=3, tiled=True)]
    all_to_all x1 -> x0, local copies, waits for them, and re-layouts: 1.26 us -> none  [per_device(): lax.all_to_all(values, 'seq', split_axis=3, concat_axis=1, tiled=True)]
    all_gather x1, waiting for transfers between devices: 0.02 us -> 1.25 us  [per_device(): lax.all_gather(value_heads, ('blk', 'chan'), axis=1, tiled=True)]
    all_to_all x1, starting transfers between devices: 3.4 us -> 4.6 us  [per_device(): lax.all_to_all(attended, 'seq', split_axis=1, concat_axis=3, tiled=True)]
  transfers between devices with their start and end apart: 5 -> 5, of which waited for: 3 -> 4; matrix products, arithmetic and copies ran while one was open for 20% -> 13% of each run, Pallas kernels for 0% -> 0%
where the time goes in v1:
time: 109 us; the launch traced here: 108 us
  blocking collectives  38.8 us (36%)
  local copies, waits for them, and re-layouts  26.7 us (24%)
  between operations  13.7 us (13%)
  waiting for transfers between devices  11.3 us (10%)
  starting transfers between devices  7.85 us (7%)
  matrix products  7.01 us (6%)
  other arithmetic  2.29 us (2%)
    all_to_all x1, blocking collectives, per_device(): lax.all_to_all(keys, 'seq', split_axis=3, concat_axis=1, tiled=True)  15 us
    unnamed x23, local copies, waits for them, and re-layouts  14.7 us
    all_to_all x1, blocking collectives, per_device(): lax.all_to_all(queries, 'seq', split_axis=3, concat_axis=1, tiled=True)  11 us
    all_to_all x1, blocking collectives, per_device(): lax.all_to_all(jnp.stack(jnp.split(values, lax.axis_size('seq'), axis=3))...  11 us
    all_to_all x1, waiting for transfers between devices, per_device(): lax.all_to_all(attended, 'seq', split_axis=1, concat_axis=3, tiled=True)  5.68 us
    all_to_all x1, starting transfers between devices, per_device(): lax.all_to_all(attended, 'seq', split_axis=1, concat_axis=3, tiled=True)  4.6 us
    ppermute x1, waiting for transfers between devices, with_halo(): lax.ppermute(head, axis, [((i + 1) % count, i) for i in range(ends)])  4.21 us
    slice x2, local copies, waits for them, and re-layouts, conv_valid(): flat_kernel = kernel[row_tap].reshape(3 * kernel.shape[2], kernel.shape[3])  3.61 us
  transfers between devices with their start and end apart: 5, of which 4 were waited for; matrix products, arithmetic and copies ran while one was open for 13% of the time, Pallas kernels for 0%

profile of v1, /device:TPU:0, one launch (start us, length us, event | category | flops | bytes accessed | tf_op | source)
XLA Modules:
  0.0 107.7 jit_solution(1480210506293598384)
XLA Ops:
  6.5 4.5 %copy.27 = bf16[1,2,16,4096]{2,1,0,3:T(2,128)(2,1)S(1)} copy(bf16[1,2,16,4096]{3,2,1,0:T(8,128)(2,1)} %param.11) | data formatting | bytes 524288 | tf_op args[1]
  11.1 2.2 %reshape.136 = bf16[4,2,16384]{2,1,0:T(2,128)(2,1)S(1)} reshape(bf16[4096,1,2,16]{3,2,1,0:T(2,128)(2,1)S(1)} %bitcast.116) | data formatting | bytes 524288
  13.3 15.0 %all_to_all.44 = bf16[4,2,16384]{2,1,0:T(2,128)(2,1)S(1)} all-to-all(bf16[4,2,16384]{2,1,0:T(2,128)(2,1)S(1)} %reshape.136), channel_id=1, replica_groups=mesh['groups'=2,'seq'=4,'blk'=2,'chan'=2] {'seq'}, dimensions={0} | all-to-all | bytes 524288 | tf_op jit(solution)/shard_map/all_to_all | solution.py:82
  28.3 1.4 %reshape.137 = bf16[4096,1,2,16]{3,2,1,0:T(2,128)(2,1)S(1)} reshape(bf16[4,2,16384]{2,1,0:T(2,128)(2,1)S(1)} %all_to_all.44) | data formatting | bytes 524288
  29.8 0.0 copy-start.2
  29.8 1.3 %copy.28 = bf16[1,2,16,4,1024]{4,2,1,3,0:T(8,128)(2,1)S(1)} copy(bf16[1,2,16,4,1024]{2,1,4,3,0:T(2,128)(2,1)S(1)} %bitcast.114) | data formatting | bytes 524288 | tf_op jit(solution)/shard_map/all_to_all | solution.py:82
  31.0 0.0 copy-start.1
  31.1 0.7 copy.47
  31.8 0.0 all-gather.4.cloned.1.call-update
  31.9 0.0 all-gather.6.cloned.1.call-start
  32.0 11.0 %all_to_all.45 = bf16[4,1,2,16,1024]{4,3,2,1,0:T(8,128)(2,1)S(1)} all-to-all(bf16[4,1,2,16,1024]{4,3,2,1,0:T(8,128)(2,1)S(1)} %pad_maximum_fusion.1), channel_id=1, replica_groups=mesh['groups'=2,'seq'=4,'blk'=2,'chan'=2] {'seq'}, dimensions={0} | all-to-all | bytes 524288 | tf_op jit(solution)/shard_map/all_to_all | solution.py:84
  43.0 0.7 copy.46
  43.8 0.0 all-gather.6.cloned.1.call-update
  43.8 2.7 %copy.24 = bf16[1,2,16,4096]{2,1,0,3:T(2,128)(2,1)S(1)} copy(bf16[1,2,16,4096]{3,2,1,0:T(8,128)(2,1)S(1)} %copy-done.1) | data formatting | bytes 524288 | tf_op args[0]
  46.5 2.2 %reshape.138 = bf16[4,2,16384]{2,1,0:T(2,128)(2,1)S(1)} reshape(bf16[4096,1,2,16]{3,2,1,0:T(2,128)(2,1)S(1)} %bitcast.117) | data formatting | bytes 524288
  48.7 11.0 %all_to_all.46 = bf16[4,2,16384]{2,1,0:T(2,128)(2,1)S(1)} all-to-all(bf16[4,2,16384]{2,1,0:T(2,128)(2,1)S(1)} %reshape.138), channel_id=1, replica_groups=mesh['groups'=2,'seq'=4,'blk'=2,'chan'=2] {'seq'}, dimensions={0} | all-to-all | bytes 524288 | tf_op jit(solution)/shard_map/all_to_all | solution.py:81
  59.7 1.4 %reshape.139 = bf16[4096,1,2,16]{3,2,1,0:T(2,128)(2,1)S(1)} reshape(bf16[4,2,16384]{2,1,0:T(2,128)(2,1)S(1)} %all_to_all.46) | data formatting | bytes 524288
  61.2 1.3 %copy.25 = bf16[1,2,16,4,1024]{4,2,1,3,0:T(8,128)(2,1)S(1)} copy(bf16[1,2,16,4,1024]{2,1,4,3,0:T(2,128)(2,1)S(1)} %bitcast.115) | data formatting | bytes 524288 | tf_op jit(solution)/shard_map/all_to_all | solution.py:81
  62.5 0.0 all-gather.4.cloned.1.call-done
  62.5 1.8 %multiply_reduce_fusion = (f32[8,128]{1,0:T(8,128)S(1)}, f32[8,128,512]{2,1,0:T(8,128)S(1)}) fusion(bf16[8,512,128]{2,1,0:T(8,128)(2,1)} %all-gather.4.cloned.1.call-done, bf16[128,8,128]{2,1,0:T(8,128)(2,1)S(1)} %bitcast.129), kind=kOutput, calls=%fused_computation.1 | convolution fusion | flops 135265280 | bytes 3411968 | tf_op jit(solution)/shard_map/hqd,hkd->hqk/dot_general | solution.py:50
  64.3 0.6 fusion
  64.9 1.3 %all-gather.6.cloned.1.call-done = bf16[8,512,128]{2,1,0:T(8,128)(2,1)} async-done(((bf16[8,128,128]{2,1,0:T(8,128)(2,1)}), bf16[8,512,128]{2,1,0:T(8,128)(2,1)}) %all-gather.6.cloned.1.call-update) | async-done | bytes 1048592 | tf_op jit(solution)/shard_map/all_gather | solution.py:122
  66.1 1.9 %fusion.4 = bf16[128,8,128]{2,0,1:T(8,128)(2,1)S(1)} fusion(bf16[8,512,128]{2,1,0:T(8,128)(2,1)} %all-gather.6.cloned.1.call-done, f32[8,128,512]{2,1,0:T(8,128)S(1)} %get-tuple-element.22, f32[8,128]{1,0:T(8,128)S(1)} %get-tuple-element.20, f32[128,8]{0,1:T(8,128)S(1)} %bitcast_add_fusion, f32[128,8]{0,1:T(8,128)S(1)} %get-tuple-element.19), kind=kOutput, calls=%fused_computation.7 | convolution fusion | flops 136183808 | bytes 3420160 | tf_op jit(solution)/shard_map/hqk,hkd->hqd/dot_general | solution.py:57
  68.0 0.2 copy.31
  68.2 0.8 reshape.119
  69.0 4.6 %all-to-all-start.3 = ((bf16[1,8,16,1024]{3,2,0,1:T(8,128)(2,1)}), bf16[1,8,16,1024]{3,2,0,1:T(8,128)(2,1)S(1)}, u32[]{:S(2)}, u32[]{:S(2)}) async-start(bf16[1,8,16,1024]{3,2,0,1:T(8,128)(2,1)} %bitcast.14), calls=%async_computation.3 | async-start | bytes 524288 | tf_op jit(solution)/shard_map/all_to_all | solution.py:127
  73.6 1.8 %fusion.30 = (bf16[1,3,64,512]{3,2,1,0:T(8,128)(2,1)}, bf16[1,3,64,512]{3,2,1,0:T(8,128)(2,1)S(1)}, bf16[1,3,64,512]{3,2,1,0:T(8,128)(2,1)S(1)}) fusion(bf16[3,3,64,512]{3,2,1,0:T(8,128)(2,1)} %param.16), kind=kLoop, calls=%fused_computation.65 | loop fusion | bytes 1179648 | tf_op jit(solution)/shard_map/slice | solution.py:36
  75.5 1.8 %fusion.29 = (bf16[1,3,512,256]{3,2,1,0:T(8,128)(2,1)S(1)}, bf16[1,3,512,256]{3,2,1,0:T(8,128)(2,1)S(1)}, bf16[1,3,512,256]{3,2,1,0:T(8,128)(2,1)S(1)}) fusion(bf16[3,3,512,256]{3,2,1,0:T(8,128)(2,1)} %param.18), kind=kLoop, calls=%fused_computation.64 | loop fusion | bytes 4718592 | tf_op jit(solution)/shard_map/slice | solution.py:36
  77.2 0.0 copy-start.4
  77.2 5.7 %all-to-all-done.3 = bf16[1,8,16,1024]{3,2,0,1:T(8,128)(2,1)S(1)} async-done(((bf16[1,8,16,1024]{3,2,0,1:T(8,128)(2,1)}), bf16[1,8,16,1024]{3,2,0,1:T(8,128)(2,1)S(1)}, u32[]{:S(2)}, u32[]{:S(2)}) %all-to-all-start.3) | async-done | bytes 262176 | tf_op jit(solution)/shard_map/all_to_all | solution.py:127
  83.0 1.1 %copy.34 = f32[1,2,16,4,1024]{4,3,2,1,0:T(4,128)} copy(f32[1,2,16,4,1024]{4,2,1,3,0:T(8,128)S(1)} %bitcast.121) | data formatting | bytes 1048576 | tf_op jit(solution)/shard_map/convert_element_type | solution.py:128
  84.1 2.2 %reshape.126 = f32[2,16,4096]{2,1,0:T(8,128)} reshape(f32[1,2,16,4,1024]{4,3,2,1,0:T(4,128)} %copy.34) | data formatting | bytes 1048576 | tf_op jit(solution)/shard_map/convert_element_type | solution.py:128
  86.3 0.7 multiply_reduce_fusion.1
  87.0 0.7 reduce_sum.31
  87.8 1.4 %fusion.10 = bf16[2,16,64]{2,1,0:T(8,128)(2,1)S(1)} fusion(bf16[4096,64]{0,1:T(8,128)(2,1)S(1)} %copy-done, f32[2,16,4096]{2,1,0:T(8,128)} %reshape.126, f32[4096]{0:T(1024)S(1)} %copy-done.4, f32[64]{0:T(128)} %param.15, f32[2,16]{1,0:T(2,128)S(1)} %add_sqrt_fusion), kind=kOutput, calls=%fused_computation.18 | convolution fusion | flops 17045504 | bytes 1069440 | tf_op jit(solution)/shard_map/frcd,dl->frcl/dot_general | solution.py:131
  89.2 1.8 %all-gather = bf16[2,32,64]{2,1,0:T(8,128)(2,1)S(1)} all-gather(bf16[2,16,64]{2,1,0:T(8,128)(2,1)S(1)} %fusion.10), channel_id=2, replica_groups=mesh['groups'=2,'seq'=4,'blk'=2,'chan'=2] {'chan'}, dimensions={1}, use_global_device_ids=true | all-gather | bytes 12288 | tf_op jit(solution)/shard_map/all_gather | solution.py:134
  91.0 1.9 %collective-permute-start = (bf16[1,2,32,64]{3,2,1,0:T(8,128)(2,1)S(1)}, bf16[1,2,32,64]{3,2,1,0:T(8,128)(2,1)S(1)}, u32[]{:S(2)}, u32[]{:S(2)}) collective-permute-start(bf16[1,2,32,64]{3,2,1,0:T(8,128)(2,1)S(1)} %bitcast.133), channel_id=1, source_target_pairs={{0,4},{4,8},{8,12},{1,5},{5,9},{9,13},{2,6},{6,10},{10,14},{3,7},{... | collective-permute-start | bytes 24584 | tf_op jit(solution)/shard_map/ppermute | solution.py:18
  92.9 1.3 %collective-permute-start.1 = (bf16[1,2,32,64]{3,2,1,0:T(8,128)(2,1)S(1)}, bf16[1,2,32,64]{3,2,1,0:T(8,128)(2,1)S(1)}, u32[]{:S(2)}, u32[]{:S(2)}) collective-permute-start(bf16[1,2,32,64]{3,2,1,0:T(8,128)(2,1)S(1)} %bitcast.134), channel_id=1, source_target_pairs={{4,0},{8,4},{12,8},{5,1},{9,5},{13,9},{6,2},{10,6},{14,10},{7,3},{... | collective-permute-start | bytes 24584 | tf_op jit(solution)/shard_map/ppermute | solution.py:20
  94.2 0.1 collective-permute-done
  94.3 4.2 %collective-permute-done.1 = bf16[1,2,32,64]{3,2,1,0:T(8,128)(2,1)S(1)} collective-permute-done((bf16[1,2,32,64]{3,2,1,0:T(8,128)(2,1)S(1)}, bf16[1,2,32,64]{3,2,1,0:T(8,128)(2,1)S(1)}, u32[]{:S(2)}, u32[]{:S(2)}) %collective-permute-start.1) | collective-permute-done | bytes 8224 | tf_op jit(solution)/shard_map/ppermute | solution.py:20
  98.6 0.1 pad_maximum_fusion.2
  98.7 0.2 fusion.25
  98.9 0.2 convolution_add_fusion.1
  99.1 0.2 fusion.18
  99.4 0.1 pad_slice_fusion.1
  99.5 0.3 fusion.20
  99.7 0.3 convolution_add_fusion.3
  100.0 0.9 fusion.8
  (25 shorter events, 0.4 us)
Async XLA Ops:
  6.5 81.2 %copy-start = (bf16[4096,64]{0,1:T(8,128)(2,1)S(1)}, bf16[4096,64]{0,1:T(8,128)(2,1)}, u32[]{:S(2)}) copy-start(bf16[4096,64]{0,1:T(8,128)(2,1)} %param.14) | copy-start | bytes 1572868
  6.5 56.0 %all-gather.4.cloned.1.call-start = ((), (), s32[]{:S(2)}) async-start(), calls=%async_computation.4 | async-start | bytes 1310720 | tf_op jit(solution)/shard_map/all_gather | solution.py:121
  29.8 2.2 %copy-start.2 = (bf16[1,2,16,4096]{3,2,1,0:T(8,128)(2,1)S(1)}, bf16[1,2,16,4096]{3,2,1,0:T(8,128)(2,1)}, u32[]{:S(2)}) copy-start(bf16[1,2,16,4096]{3,2,1,0:T(8,128)(2,1)} %param.12) | copy-start | bytes 786436
  31.0 12.8 %copy-start.1 = (bf16[1,2,16,4096]{3,2,1,0:T(8,128)(2,1)S(1)}, bf16[1,2,16,4096]{3,2,1,0:T(8,128)(2,1)}, u32[]{:S(2)}) copy-start(bf16[1,2,16,4096]{3,2,1,0:T(8,128)(2,1)} %param.10) | copy-start | bytes 786436
  31.9 34.3 %all-gather.6.cloned.1.call-start = ((), (), s32[]{:S(2)}) async-start(), calls=%async_computation.5 | async-start | bytes 1310720 | tf_op jit(solution)/shard_map/all_gather | solution.py:122
  69.0 13.9 %all-to-all-start.3 = ((bf16[1,8,16,1024]{3,2,0,1:T(8,128)(2,1)}), bf16[1,8,16,1024]{3,2,0,1:T(8,128)(2,1)S(1)}, u32[]{:S(2)}, u32[]{:S(2)}) async-start(bf16[1,8,16,1024]{3,2,0,1:T(8,128)(2,1)} %bitcast.14), calls=%async_computation.3 | async-start | bytes 524288 | tf_op jit(solution)/shard_map/all_to_all | solution.py:127
  77.2 10.6 %copy-start.4 = (f32[4096]{0:T(1024)S(1)}, f32[4096]{0:T(1024)}, u32[]{:S(2)}) copy-start(f32[4096]{0:T(1024)} %param.13) | copy-start | bytes 49156
  87.0 12.0 %copy-start.6 = (f32[512]{0:T(512)S(1)}, f32[512]{0:T(512)}, u32[]{:S(2)}) copy-start(f32[512]{0:T(512)} %param.17) | copy-start | bytes 6148
  87.8 11.3 %copy-start.3 = (bf16[1,3,64,512]{3,2,1,0:T(8,128)(2,1)S(1)}, bf16[1,3,64,512]{3,2,1,0:T(8,128)(2,1)}, u32[]{:S(2)}) copy-start(bf16[1,3,64,512]{3,2,1,0:T(8,128)(2,1)} %get-tuple-element.8) | copy-start | bytes 589828
  91.0 3.4 %collective-permute-start = (bf16[1,2,32,64]{3,2,1,0:T(8,128)(2,1)S(1)}, bf16[1,2,32,64]{3,2,1,0:T(8,128)(2,1)S(1)}, u32[]{:S(2)}, u32[]{:S(2)}) collective-permute-start(bf16[1,2,32,64]{3,2,1,0:T(8,128)(2,1)S(1)} %bitcast.133), channel_id=1, source_target_pairs={{0,4},{4,8},{8,12},{1,5},{5,9},{9,13},{2,6},{6,10},{10,14},{3,7},{... | collective-permute-start | bytes 24584 | tf_op jit(solution)/shard_map/ppermute | solution.py:18
  92.9 5.6 %collective-permute-start.1 = (bf16[1,2,32,64]{3,2,1,0:T(8,128)(2,1)S(1)}, bf16[1,2,32,64]{3,2,1,0:T(8,128)(2,1)S(1)}, u32[]{:S(2)}, u32[]{:S(2)}) collective-permute-start(bf16[1,2,32,64]{3,2,1,0:T(8,128)(2,1)S(1)} %bitcast.134), channel_id=1, source_target_pairs={{4,0},{8,4},{12,8},{5,1},{9,5},{13,9},{6,2},{10,6},{14,10},{7,3},{... | collective-permute-start | bytes 24584 | tf_op jit(solution)/shard_map/ppermute | solution.py:20
  99.1 0.9 copy-start.5
Sparse Core Ops, SparseCore 0:
  32.0 15.7 all-gather.3
  49.4 16.6 all-gather.5
